TPU v7x, 128 devices: a whole 4x4x4 slice. The times are simulated.
128 devices in a mesh: dp: 8 (over z_lo, y), sp: 16 (over x, z_hi, core).
Axes of the slice: x: 4, y: 4, z: 4 (z_hi: 2, z_lo: 2; z = z_hi * 2 + z_lo), core: 2. Of those that a mesh axis runs over, the one named last changes fastest.
Arguments:
- feats: bfloat16 [8, 32, 256, 128], P('dp', None, 'sp'), may hold values from -62 to 62
- conv_w: bfloat16 [1152, 256], replicated, may hold values from -0.1875 to 0.1875
- group_norm_gain: float32 [256], replicated, may hold values from 0.5 to 1.5
- group_norm_bias: float32 [256], replicated, may hold values from -3 to 3
- emb_w: bfloat16 [256, 3072], replicated, may hold values from -0.375 to 0.375
- time_w: bfloat16 [256, 9216], replicated, may hold values from -0.375 to 0.375
- up_w: bfloat16 [3072, 6144], P(None, 'sp'), may hold values from -0.109375 to 0.109375
- down_w: bfloat16 [6144, 3072], P('sp'), may hold values from -0.078125 to 0.078125
- steps: int32 [8], P('dp'), may hold values from 0 to 999
- cotangent: bfloat16 [8, 2048, 3072], P('dp', 'sp'), may hold values from -28 to 28
Outputs:
- grad_conv: float32 [1152, 256], replicated
- grad_up: float32 [3072, 6144], P('dp', 'sp')
- grad_down: float32 [6144, 3072], P('sp', 'dp')
All inputs are finite; a program needn't handle non-finite values.
Results may differ from a plain program's by a relative error of at most 0.012.
Values may be sent and summed in bfloat16 or wider, within the bound.
A program may use at most 192 MiB of HBM per device.

v0:
```python
import math
import jax
import jax.numpy as jnp
from jax import lax
from jax.sharding import Mesh
from jax.sharding import PartitionSpec as P

NORM_GROUPS = 32
SP = ("sp_0", "sp_1", "sp_2")
DP_SP = ("dp", "sp_0", "sp_1", "sp_2")


def from_behind(array, axis, by):
    length = lax.axis_size(axis)
    pairs = [(i, i + by) for i in range(length) if 0 <= i + by < length]
    return lax.ppermute(array, axis, pairs)


def copy_for_each(array, axis):
    length = lax.axis_size(axis)
    return lax.all_to_all(
        jnp.broadcast_to(array[None], (length, *array.shape)), axis, 0, 0, tiled=True
    )


def over_copies(array, axis):
    return copy_for_each(array, axis).sum(axis=0)


def in_one(arrays, axis):
    ends = [0]
    for a in arrays:
        ends.append(ends[-1] + a.size)
    subtotal = over_copies(jnp.concatenate([a.ravel() for a in arrays]), axis)
    return tuple((subtotal[b:e].reshape(a.shape) for a, b, e in zip(arrays, ends, ends[1:])))


def side_by_side(arrays, axis, dim, along):
    both = jnp.concatenate(arrays, axis=along)
    filled, at, finished = (lax.all_gather(both, axis, axis=dim, tiled=True), 0, [])
    for a in arrays:
        finished.append(lax.slice_in_dim(filled, at, at + a.shape[along], axis=along))
        at += a.shape[along]
    return tuple(finished)


def in_blocks(array, dim, length):
    before, after = (array.shape[:dim], array.shape[dim + 1 :])
    return jnp.moveaxis(array.reshape(*before, length, -1, *after), dim, 0)


def sum_by_chip(array, chips, core, dim):
    sizes = (lax.axis_size(chips), lax.axis_size(core))
    parts = in_blocks(array, dim, sizes[0] * sizes[1])
    inside = parts.shape[1:]
    parts = parts.reshape(*sizes, *inside).swapaxes(0, 1).reshape(-1, *inside)
    parts = lax.psum_scatter(parts, core, scatter_dimension=0, tiled=True)
    return lax.psum_scatter(parts, chips, scatter_dimension=0, tiled=True)[0]


def sum_packed(arrays, axis, dims):
    length = lax.axis_size(axis)
    parts = [in_blocks(a, dim, length) for a, dim in zip(arrays, dims)]
    lines = jnp.concatenate([b.reshape(length, -1) for b in parts], axis=1)
    rows = max(16, -(-lines.shape[1] // 1024) * 8)
    lines = jnp.pad(lines, ((0, 0), (0, rows * 128 - lines.shape[1]))).reshape(-1, 128)
    ravelled, at, finished = (lax.psum_scatter(lines, axis, tiled=True).reshape(-1), 0, [])
    for b in parts:
        part = b[0]
        finished.append(ravelled[at : at + part.size].reshape(part.shape))
        at += part.size
    return tuple(finished)


def gelu_pair(u):
    coef = math.sqrt(2.0 / math.pi)
    inner = coef * (u + 0.044715 * u * u * u)
    tangent = jnp.tanh(inner)
    value = 0.5 * u * (1.0 + tangent)
    slope = 0.5 * (1.0 + tangent) + 0.5 * u * (1.0 - tangent * tangent) * coef * (
        1.0 + 3.0 * 0.044715 * u * u
    )
    return (value, slope)


def silu_pair(value):
    sigma = jax.nn.sigmoid(value)
    return (value * sigma, sigma * (1.0 + value * (1.0 - sigma)))


def modulation(step_value, time_w):
    half = time_w.shape[0] // 2
    freqs = jnp.exp(-math.log(10000.0) * jnp.arange(half, dtype=jnp.float32) / half)
    angle = step_value.astype(jnp.float32) * freqs
    embed = jnp.concatenate([jnp.cos(angle), jnp.sin(angle)])
    mixed = jnp.dot(
        jax.nn.silu(embed).astype(jnp.bfloat16)[None, :], time_w, preferred_element_type=jnp.float32
    )[0]
    width = time_w.shape[1] // 3
    return (mixed[:width], mixed[width : 2 * width], mixed[2 * width :])


def make_patches(padded, rows, cols):
    pieces = []
    for row_tap in range(3):
        for col_tap in range(3):
            pieces.append(
                padded[row_tap : row_tap + 2 * rows : 2, col_tap : col_tap + 2 * cols : 2, :]
            )
    stacked = jnp.concatenate(pieces, axis=-1)
    return stacked.reshape(rows * cols, stacked.shape[-1])


def group_totals(first, second, groups):
    tokens, width = first.shape
    first_g = first.reshape(tokens, groups, width // groups)
    second_g = second.reshape(tokens, groups, width // groups)
    return (jnp.sum(first_g, axis=(0, 2)), jnp.sum(second_g, axis=(0, 2)))


def broadcast_groups(values, width):
    return jnp.repeat(values, width // values.shape[0])


def contract(left, right, left_dim, right_dim):
    return lax.dot_general(
        left, right, (((left_dim,), (right_dim,)), ((), ())), preferred_element_type=jnp.float32
    )


def on_device(
    feats, conv_w, group_norm_gain, group_norm_bias, emb_w, time_w, up_w, down_w, steps, cotangent
):
    devices_sp = lax.axis_size(SP)
    image = feats[0]
    rows_in, cols_in, _ = image.shape
    rows = rows_in // 2
    cols = cols_in // 2
    seq_rows = rows // devices_sp
    channel_count = conv_w.shape[1]
    rim = from_behind(image[:, cols_in - 1, :], SP, 1)
    widened = jnp.concatenate([rim[:, None, :], image], axis=1)
    padded = jnp.pad(widened, ((1, 0), (0, 0), (0, 0)))
    patches = make_patches(padded, rows, cols)
    normed_value = jnp.dot(patches, conv_w, preferred_element_type=jnp.float32)
    first, second = group_totals(normed_value, normed_value * normed_value, NORM_GROUPS)
    first, second = in_one((first, second), SP)
    group_count = normed_value.shape[0] * devices_sp * (channel_count // NORM_GROUPS)
    group_mean = first / group_count
    rstd = lax.rsqrt(second / group_count - group_mean * group_mean + 1e-05)
    channel_rstd = broadcast_groups(rstd, channel_count)
    centered_input = (normed_value - broadcast_groups(group_mean, channel_count)) * channel_rstd
    preactivation = centered_input * group_norm_gain + group_norm_bias
    act_val, silu_slope = silu_pair(preactivation)
    act_b = act_val.astype(jnp.bfloat16)
    shift, scale, gate = modulation(steps[0], time_w)
    cot_seq = cotangent[0]
    moved = lax.all_to_all(
        act_b.reshape(rows, cols, channel_count), SP, split_axis=0, concat_axis=1, tiled=True
    )
    local_act = moved.reshape(seq_rows * cols * devices_sp, channel_count)
    hidden_in = jnp.dot(local_act, emb_w, preferred_element_type=jnp.float32)
    centered = hidden_in - jnp.mean(hidden_in, axis=-1, keepdims=True)
    token_rstd = lax.rsqrt(jnp.mean(centered * centered, axis=-1, keepdims=True) + 1e-06)
    hhat = centered * token_rstd
    normed = (hhat * (1.0 + scale) + shift).astype(jnp.bfloat16)
    all_normed, all_cot = side_by_side((normed, cot_seq), SP, 0, 1)
    upper = jnp.dot(all_normed, up_w, preferred_element_type=jnp.float32)
    gelu_val, gelu_slope = gelu_pair(upper)
    hid = gelu_val.astype(jnp.bfloat16)
    scaled_cot = (all_cot.astype(jnp.float32) * gate).astype(jnp.bfloat16)
    dhid = contract(scaled_cot, down_w, 1, 1)
    dupper = (dhid * gelu_slope).astype(jnp.bfloat16)
    dnormed = sum_by_chip(
        contract(dupper, up_w, 1, 1).astype(jnp.bfloat16), ("sp_0", "sp_1"), "sp_2", 0
    ).astype(jnp.float32)
    grad_up_local = contract(all_normed, dupper, 0, 0)
    grad_down_local = contract(hid, scaled_cot, 0, 0)
    grad_up, grad_down = tuple(
        (
            part.astype(jnp.float32)
            for part in sum_packed(
                (grad_up_local.astype(jnp.bfloat16), grad_down_local.astype(jnp.bfloat16)),
                "dp",
                (0, 1),
            )
        )
    )
    dhh = dnormed * (1.0 + scale)
    dhh_mean = jnp.mean(dhh, axis=-1, keepdims=True)
    dhh_cross = jnp.mean(dhh * hhat, axis=-1, keepdims=True)
    dh_val = (
        cot_seq.astype(jnp.float32) + token_rstd * (dhh - dhh_mean - hhat * dhh_cross)
    ).astype(jnp.bfloat16)
    dact = contract(dh_val, emb_w, 1, 1)
    back_tiles = lax.all_to_all(
        dact.reshape(seq_rows, cols * devices_sp, channel_count).astype(jnp.bfloat16),
        SP,
        split_axis=1,
        concat_axis=0,
        tiled=True,
    ).astype(jnp.float32)
    dact_tile = back_tiles.reshape(rows * cols, channel_count)
    input_gradient = dact_tile * silu_slope * group_norm_gain
    backward_first, backward_second = group_totals(
        input_gradient, input_gradient * centered_input, NORM_GROUPS
    )
    backward_first, backward_second = in_one((backward_first, backward_second), SP)
    normed_gradient = (
        channel_rstd
        * (
            input_gradient
            - broadcast_groups(backward_first / group_count, channel_count)
            - centered_input * broadcast_groups(backward_second / group_count, channel_count)
        )
    ).astype(jnp.bfloat16)
    conv_local = contract(patches, normed_gradient, 0, 0)
    grad_conv = lax.psum(conv_local, DP_SP)
    return (grad_conv, grad_up, grad_down)


def solution(mesh):
    finer = Mesh(mesh.devices.reshape(mesh.shape["dp"], 4, 2, 2), ("dp", "sp_0", "sp_1", "sp_2"))
    in_specs = (
        P("dp", None, SP, None),
        P(),
        P(),
        P(),
        P(),
        P(),
        P(None, SP),
        P(SP, None),
        P("dp"),
        P("dp", SP, None),
    )
    out_specs = (P(), P("dp", SP), P(SP, "dp"))
    return jax.shard_map(
        on_device, mesh=finer, in_specs=in_specs, out_specs=out_specs, check_vma=False
    )
```

profile of v0, /device:TPU:1, one launch (start us, length us, event | category | flops | bytes accessed | tf_op | source)
XLA Modules:
  0.0 589.0 jit_solution(9743201290991420241)
XLA Ops:
  8.3 6.9 %collective-permute-start = (bf16[32,128]{1,0:T(8,128)(2,1)S(1)}, bf16[32,128]{1,0:T(8,128)(2,1)S(1)}, u32[]{:S(2)}, u32[]{:S(2)}) collective-permute-start(bf16[32,128]{1,0:T(8,128)(2,1)S(1)} %slice_bitcast_fusion), channel_id=1, source_target_pairs={{0,1},{1,2},{2,3},{3,4},{4,5},{5,6},{6,7},{7,8},{8,9},{9,10},{10,1... | collective-permute-start | bytes 24584 | tf_op jit(solution)/shard_map/ppermute | solution.py:16
  21.0 7.9 %all-to-all-start = ((f32[16,1,64]{2,1,0:T(1,128)}), f32[16,1,64]{2,1,0:T(1,128)S(1)}, u32[]{:S(2)}, u32[]{:S(2)}) async-start(f32[16,1,64]{2,1,0:T(1,128)} %broadcast_in_dim.15), calls=%async_computation | async-start | bytes 16384 | tf_op jit(solution)/shard_map/all_to_all | solution.py:21
  29.0 3.1 fusion.66
  32.0 3.9 all-to-all-done
  37.0 4.0 all-to-all-start.1
  41.0 7.4 %all-to-all-done.1 = bf16[16,8,256]{2,1,0:T(8,128)(2,1)S(1)} async-done(((bf16[16,8,256]{2,1,0:T(8,128)(2,1)}), bf16[16,8,256]{2,1,0:T(8,128)(2,1)S(1)}, u32[]{:S(2)}, u32[]{:S(2)}) %all-to-all-start.1) | async-done | bytes 65568 | tf_op jit(solution)/shard_map/all_to_all | solution.py:158
  48.4 1.9 fusion.65
  53.5 146.6 %all-gather.2.cloned.1.call-done = bf16[2048,6144]{1,0:T(8,128)(2,1)} async-done(((bf16[128,6144]{1,0:T(8,128)(2,1)}), bf16[2048,6144]{1,0:T(8,128)(2,1)}) %all-gather.2.cloned.1.call-update) | async-done | bytes 25165840 | tf_op jit(solution)/shard_map/all_gather | solution.py:40
  200.1 9.7 %fusion.2 = f32[2048,384]{1,0:T(8,128)S(1)} fusion(bf16[3072,384]{1,0:T(8,128)(2,1)S(1)} %copy-done, bf16[2048,6144]{1,0:T(8,128)(2,1)} %all-gather.2.cloned.1.call-done), kind=kOutput, calls=%fused_computation.4 | convolution fusion | flops 4831838208 | bytes 18087936 | tf_op jit(solution)/shard_map/dot_general | solution.py:168
  209.9 12.3 %fusion.16 = bf16[2048,384]{1,0:T(8,128)(2,1)S(1)} fusion(f32[2048,384]{1,0:T(8,128)S(1)} %fusion.2, bf16[384,3072]{1,0:T(8,128)(2,1)S(1)} %copy-done.8, bf16[2048,6144]{1,0:T(8,128)(2,1)} %all-gather.2.cloned.1.call-done, f32[3072]{0:T(1024)S(1)} %get-tuple-element.12), kind=kOutput, calls=%fused_computation.19 | convolution fusion | flops 4865654784 | bytes 19673088 | tf_op jit(solution)/shard_map/dot_general | solution.py:126
  222.2 7.0 %convolution_convert_fusion = bf16[2048,3072]{1,0:T(8,128)(2,1)S(1)} fusion(bf16[2048,384]{1,0:T(8,128)(2,1)S(1)} %fusion.16, bf16[3072,384]{1,0:T(8,128)(2,1)S(1)} %copy-done), kind=kOutput, calls=%fused_computation.1 | convolution fusion | flops 4838129664 | bytes 16515072 | tf_op jit(solution)/shard_map/dot_general | solution.py:126
  229.3 5.4 copy.33
  236.0 10.8 %fusion.7 = bf16[3072,384]{1,0:T(8,128)(2,1)} fusion(bf16[2048,384]{1,0:T(8,128)(2,1)S(1)} %copy-done.10, bf16[2048,6144]{1,0:T(8,128)(2,1)} %all-gather.2.cloned.1.call-done), kind=kOutput, calls=%fused_computation.12 | convolution fusion | flops 4833017856 | bytes 16515072 | tf_op jit(solution)/shard_map/dot_general | solution.py:126
  246.8 3.2 reshape_reshape.7
  250.0 13.4 %fusion.6 = bf16[384,3072]{1,0:T(8,128)(2,1)S(1)} fusion(bf16[2048,6144]{1,0:T(8,128)(2,1)} %all-gather.2.cloned.1.call-done, f32[3072]{0:T(1024)S(1)} %get-tuple-element.12, f32[2048,384]{1,0:T(8,128)} %copy-done.11), kind=kOutput, calls=%fused_computation.11 | convolution fusion | flops 4858970112 | bytes 18100224 | tf_op jit(solution)/shard_map/dot_general | solution.py:126
  265.7 10.4 %pad_maximum_fusion = bf16[8,294912]{1,0:T(8,128)(2,1)} fusion(bf16[8,147456]{1,0:T(8,128)(2,1)} %bitcast.67, bf16[8,147456]{1,0:T(8,128)(2,1)S(1)} %reshape_reshape.7), kind=kLoop, calls=%fused_computation.10 | loop fusion | flops 9437184 | bytes 9437184 | tf_op jit(solution)/shard_map/concatenate | solution.py:64
  276.1 6.6 %reshape.118 = bf16[18432,128]{1,0:T(8,128)(2,1)} reshape(bf16[8,294912]{1,0:T(8,128)(2,1)} %pad_maximum_fusion) | data formatting | bytes 9437184 | tf_op jit(solution)/shard_map/reshape | solution.py:66
  282.8 79.5 %reduce-scatter.6.cloned.1.call-done = bf16[1,128,3072]{2,1,0:T(8,128)(2,1)} async-done(((bf16[8,128,3072]{2,1,0:T(8,128)(2,1)}), bf16[1,128,3072]{2,1,0:T(8,128)(2,1)}) %reduce-scatter.6.cloned.1.call-update) | async-done | bytes 786448 | tf_op jit(solution)/shard_map/reduce_scatter | solution.py:58
  364.0 2.5 fusion.29
  368.1 12.2 %all_to_all.30 = bf16[16,2,1024]{2,1,0:T(2,128)(2,1)S(1)} all-to-all(bf16[16,2,1024]{2,1,0:T(2,128)(2,1)S(1)} %reshape.125), channel_id=1, replica_groups=mesh['dp'=8,'sp_0'=4,'sp_1'=2,'sp_2'=2] {'sp_0','sp_1','sp_2'}, dimensions={0} | all-to-all | bytes 131072 | tf_op jit(solution)/shard_map/all_to_all | solution.py:196
  381.0 10.0 %all_to_all.31 = f32[16,1,64]{2,1,0:T(1,128)S(1)} all-to-all(f32[16,1,64]{2,1,0:T(1,128)S(1)} %broadcast_in_dim.18), channel_id=1, replica_groups=mesh['dp'=8,'sp_0'=4,'sp_1'=2,'sp_2'=2] {'sp_0','sp_1','sp_2'}, dimensions={0} | all-to-all | bytes 8192 | tf_op jit(solution)/shard_map/all_to_all | solution.py:21
  392.9 29.4 %reduce-scatter.8.cloned.1.call-done = bf16[2304,128]{1,0:T(8,128)(2,1)} async-done(((bf16[18432,128]{1,0:T(8,128)(2,1)}), bf16[2304,128]{1,0:T(8,128)(2,1)}) %reduce-scatter.8.cloned.1.call-update) | async-done | bytes 589840 | tf_op jit(solution)/shard_map/reduce_scatter | solution.py:67
  425.3 154.8 %all-reduce.3.cloned.1.call-done = f32[1152,256]{1,0:T(8,128)} async-done(((f32[1152,256]{1,0:T(8,128)}), f32[1152,256]{1,0:T(8,128)}) %all-reduce.3.cloned.1.call-update) | async-done | bytes 1179664 | tf_op jit(solution)/shard_map/psum | solution.py:218
  580.2 2.4 copy.64
  (106 shorter events, 22.9 us)
Async XLA Ops:
  7.2 193.0 %copy-start = (bf16[3072,384]{1,0:T(8,128)(2,1)S(1)}, bf16[3072,384]{1,0:T(8,128)(2,1)}, u32[]{:S(2)}) copy-start(bf16[3072,384]{1,0:T(8,128)(2,1)} %param.16) | copy-start | bytes 7077892
  8.3 7.7 %collective-permute-start = (bf16[32,128]{1,0:T(8,128)(2,1)S(1)}, bf16[32,128]{1,0:T(8,128)(2,1)S(1)}, u32[]{:S(2)}, u32[]{:S(2)}) collective-permute-start(bf16[32,128]{1,0:T(8,128)(2,1)S(1)} %slice_bitcast_fusion), channel_id=1, source_target_pairs={{0,1},{1,2},{2,3},{3,4},{4,5},{5,6},{6,7},{7,8},{8,9},{9,10},{10,1... | collective-permute-start | bytes 24584 | tf_op jit(solution)/shard_map/ppermute | solution.py:16
  18.5 17.8 %copy-start.6 = (f32[256]{0:T(256)S(1)}, f32[256]{0:T(256)}, u32[]{:S(2)}) copy-start(f32[256]{0:T(256)} %param.13) | copy-start | bytes 3076
  18.5 17.8 %copy-start.7 = (f32[256]{0:T(256)S(1)}, f32[256]{0:T(256)}, u32[]{:S(2)}) copy-start(f32[256]{0:T(256)} %param.12) | copy-start | bytes 3076
  21.0 14.8 %all-to-all-start = ((f32[16,1,64]{2,1,0:T(1,128)}), f32[16,1,64]{2,1,0:T(1,128)S(1)}, u32[]{:S(2)}, u32[]{:S(2)}) async-start(f32[16,1,64]{2,1,0:T(1,128)} %broadcast_in_dim.15), calls=%async_computation | async-start | bytes 16384 | tf_op jit(solution)/shard_map/all_to_all | solution.py:21
  37.0 11.4 %all-to-all-start.1 = ((bf16[16,8,256]{2,1,0:T(8,128)(2,1)}), bf16[16,8,256]{2,1,0:T(8,128)(2,1)S(1)}, u32[]{:S(2)}, u32[]{:S(2)}) async-start(bf16[16,8,256]{2,1,0:T(8,128)(2,1)} %fusion.52), calls=%async_computation.1 | async-start | bytes 131072 | tf_op jit(solution)/shard_map/all_to_all | solution.py:158
  41.0 159.2 %all-gather.2.cloned.1.call-start = ((), (), s32[]{:S(2)}) async-start(), calls=%async_computation.7 | async-start | bytes 26738688 | tf_op jit(solution)/shard_map/all_gather | solution.py:40
  48.4 3.5 copy-start.4
  50.4 1.2 copy-start.2
  53.3 212.1 %reduce-scatter.4.cloned.1.call-start = ((), (), s32[]{:S(2)}) async-start(), calls=%async_computation.8 | async-start | bytes 18874368 | tf_op jit(solution)/shard_map/reduce_scatter | solution.py:57
  200.1 9.8 %copy-start.8 = (bf16[384,3072]{1,0:T(8,128)(2,1)S(1)}, bf16[384,3072]{1,0:T(8,128)(2,1)}, u32[]{:S(2)}) copy-start(bf16[384,3072]{1,0:T(8,128)(2,1)} %param.17) | copy-start | bytes 7077892
  209.9 12.3 %copy-start.11 = (f32[2048,384]{1,0:T(8,128)}, f32[2048,384]{1,0:T(8,128)S(1)}, u32[]{:S(2)}) copy-start(f32[2048,384]{1,0:T(8,128)S(1)} %fusion.2) | copy-start | bytes 9437188
  222.2 7.0 %copy-start.9 = (bf16[2048,384]{1,0:T(8,128)(2,1)}, bf16[2048,384]{1,0:T(8,128)(2,1)S(1)}, u32[]{:S(2)}) copy-start(bf16[2048,384]{1,0:T(8,128)(2,1)S(1)} %fusion.16) | copy-start | bytes 4718596
  234.6 1.4 copy-start.10
  234.6 127.7 %reduce-scatter.6.cloned.1.call-start = ((), (), s32[]{:S(2)}) async-start(), calls=%async_computation.9 | async-start | bytes 7077888 | tf_op jit(solution)/shard_map/reduce_scatter | solution.py:58
  265.4 156.9 %reduce-scatter.8.cloned.1.call-start = ((), (), s32[]{:S(2)}) async-start(), calls=%async_computation.11 | async-start | bytes 5308416 | tf_op jit(solution)/shard_map/reduce_scatter | solution.py:67
  282.7 79.6 %copy-start.3 = (f32[128,3072]{1,0:T(8,128)S(1)}, f32[128,3072]{1,0:T(8,128)}, u32[]{:S(2)}) copy-start(f32[128,3072]{1,0:T(8,128)} %copy-done.2) | copy-start | bytes 4718596
  282.7 81.2 %copy-start.5 = (bf16[1,128,3072]{2,1,0:T(8,128)(2,1)S(1)}, bf16[1,128,3072]{2,1,0:T(8,128)(2,1)}, u32[]{:S(2)}) copy-start(bf16[1,128,3072]{2,1,0:T(8,128)(2,1)} %param.19) | copy-start | bytes 2359300
  282.7 297.4 %all-reduce.3.cloned.1.call-start = ((), (), s32[]{:S(2)}) async-start(), calls=%async_computation.10 | async-start | bytes 2359296 | tf_op jit(solution)/shard_map/psum | solution.py:218
  392.8 189.7 %copy-start.1 = (bf16[3072,384]{1,0:T(8,128)(2,1)S(1)}, bf16[3072,384]{1,0:T(8,128)(2,1)}, u32[]{:S(2)}) copy-start(bf16[3072,384]{1,0:T(8,128)(2,1)} %param.16) | copy-start | bytes 7077892
Sparse Core Ops, SparseCore 0:
  53.4 146.6 all-gather.1
  234.8 21.5 reduce-scatter.3
  265.5 96.7 reduce-scatter.5
  364.7 57.5 reduce-scatter.7
  428.2 151.9 all-reduce.2
where the time goes:
time: 590 us; the launch traced here: 589 us
  waiting for transfers between devices  422 us (72%)
  matrix products  63.3 us (11%)
  local copies, waits for them, and re-layouts  29.3 us (5%)
  blocking collectives  22.2 us (4%)
  starting transfers between devices  19.6 us (3%)
  other arithmetic  17.9 us (3%)
  between operations  14.8 us (3%)
    psum x1, waiting for transfers between devices, on_device(): grad_conv = lax.psum(conv_local, DP_SP)  155 us
    all_gather x1, waiting for transfers between devices, side_by_side(): lax.all_gather(both, axis, axis=dim, tiled=True)  147 us
    reduce_scatter x1, waiting for transfers between devices, sum_by_chip(): return lax.psum_scatter(parts, chips, scatter_dimension=0, tiled=True)[0]  79.5 us
    dot_general x6, matrix products, contract(): lax.dot_general(left, right, (((left_dim,), (right_dim,)), ((), ())), pre...  47.3 us
    reduce_scatter x1, waiting for transfers between devices, sum_packed(): lax.psum_scatter(lines, axis, tiled=True).reshape(-1)  29.4 us
    all_to_all x1, blocking collectives, on_device(): lax.all_to_all(dact.reshape(seq_rows, cols * devices_sp, channel_count).a...  12.2 us
  transfers between devices with their start and end apart: 8, of which 6 were waited for; matrix products, arithmetic and copies ran while one was open for 10% of the time, Pallas kernels for 0%

commit v1 on v0

--- a/solution.py
+++ b/solution.py
@@ -193,12 +193,20 @@
         cot_seq.astype(jnp.float32) + token_rstd * (dhh - dhh_mean - hhat * dhh_cross)
     ).astype(jnp.bfloat16)
     dact = contract(dh_val, emb_w, 1, 1)
-    back_tiles = lax.all_to_all(
-        dact.reshape(seq_rows, cols * devices_sp, channel_count).astype(jnp.bfloat16),
-        SP,
-        split_axis=1,
-        concat_axis=0,
-        tiled=True,
+    back_tiles = jnp.concatenate(
+        lax.all_to_all(
+            jnp.stack(
+                jnp.split(
+                    dact.reshape(seq_rows, cols * devices_sp, channel_count).astype(jnp.bfloat16),
+                    lax.axis_size(SP),
+                    axis=1,
+                )
+            ),
+            SP,
+            0,
+            0,
+        ),
+        axis=0,
     ).astype(jnp.float32)
     dact_tile = back_tiles.reshape(rows * cols, channel_count)
     input_gradient = dact_tile * silu_slope * group_norm_gain

time: 590 us -> 589 us (level)
  no operation moved by 1% of the time
where the time goes in v1:
time: 589 us
  waiting for transfers between devices  423 us (72%)
  matrix products  63.4 us (11%)
  local copies, waits for them, and re-layouts  28.6 us (5%)
  blocking collectives  21.9 us (4%)
  starting transfers between devices  19.6 us (3%)
  other arithmetic  16.9 us (3%)
  between operations  14.9 us (3%)
    psum x1, waiting for transfers between devices, on_device(): grad_conv = lax.psum(conv_local, DP_SP)  155 us
    all_gather x1, waiting for transfers between devices, side_by_side(): lax.all_gather(both, axis, axis=dim, tiled=True)  147 us
    reduce_scatter x1, waiting for transfers between devices, sum_by_chip(): return lax.psum_scatter(parts, chips, scatter_dimension=0, tiled=True)[0]  79.7 us
    dot_general x6, matrix products, contract(): lax.dot_general(left, right, (((left_dim,), (right_dim,)), ((), ())), pre...  47.3 us
    reduce_scatter x1, waiting for transfers between devices, sum_packed(): lax.psum_scatter(lines, axis, tiled=True).reshape(-1)  31.1 us
    all_to_all x1, blocking collectives, on_device(): lax.all_to_all(jnp.stack(jnp.split(dact.reshape(seq_rows, cols * devices_...  11.9 us
  transfers between devices with their start and end apart: 8, of which 6 were waited for; matrix products, arithmetic and copies ran while one was open for 10% of the time, Pallas kernels for 0%

profile of v1, /device:TPU:1, one launch (start us, length us, event | category | flops | bytes accessed | tf_op | source)
XLA Modules:
  0.0 588.8 jit_solution(800800306029763828)
XLA Ops:
  8.3 6.9 %collective-permute-start = (bf16[32,128]{1,0:T(8,128)(2,1)S(1)}, bf16[32,128]{1,0:T(8,128)(2,1)S(1)}, u32[]{:S(2)}, u32[]{:S(2)}) collective-permute-start(bf16[32,128]{1,0:T(8,128)(2,1)S(1)} %slice_bitcast_fusion), channel_id=1, source_target_pairs={{0,1},{1,2},{2,3},{3,4},{4,5},{5,6},{6,7},{7,8},{8,9},{9,10},{10,1... | collective-permute-start | bytes 24584 | tf_op jit(solution)/shard_map/ppermute | solution.py:16
  21.0 7.9 %all-to-all-start = ((f32[16,1,64]{2,1,0:T(1,128)}), f32[16,1,64]{2,1,0:T(1,128)S(1)}, u32[]{:S(2)}, u32[]{:S(2)}) async-start(f32[16,1,64]{2,1,0:T(1,128)} %broadcast_in_dim.15), calls=%async_computation | async-start | bytes 16384 | tf_op jit(solution)/shard_map/all_to_all | solution.py:21
  29.0 3.1 fusion.66
  32.0 3.9 all-to-all-done
  37.0 4.0 all-to-all-start.1
  41.0 7.4 %all-to-all-done.1 = bf16[16,8,256]{2,1,0:T(8,128)(2,1)S(1)} async-done(((bf16[16,8,256]{2,1,0:T(8,128)(2,1)}), bf16[16,8,256]{2,1,0:T(8,128)(2,1)S(1)}, u32[]{:S(2)}, u32[]{:S(2)}) %all-to-all-start.1) | async-done | bytes 65568 | tf_op jit(solution)/shard_map/all_to_all | solution.py:158
  48.4 1.9 fusion.65
  53.5 146.6 %all-gather.2.cloned.1.call-done = bf16[2048,6144]{1,0:T(8,128)(2,1)} async-done(((bf16[128,6144]{1,0:T(8,128)(2,1)}), bf16[2048,6144]{1,0:T(8,128)(2,1)}) %all-gather.2.cloned.1.call-update) | async-done | bytes 25165840 | tf_op jit(solution)/shard_map/all_gather | solution.py:40
  200.1 9.8 %fusion.2 = f32[2048,384]{1,0:T(8,128)S(1)} fusion(bf16[3072,384]{1,0:T(8,128)(2,1)S(1)} %copy-done, bf16[2048,6144]{1,0:T(8,128)(2,1)} %all-gather.2.cloned.1.call-done), kind=kOutput, calls=%fused_computation.4 | convolution fusion | flops 4831838208 | bytes 18087936 | tf_op jit(solution)/shard_map/dot_general | solution.py:168
  209.9 12.3 %fusion.16 = bf16[2048,384]{1,0:T(8,128)(2,1)S(1)} fusion(f32[2048,384]{1,0:T(8,128)S(1)} %fusion.2, bf16[384,3072]{1,0:T(8,128)(2,1)S(1)} %copy-done.8, bf16[2048,6144]{1,0:T(8,128)(2,1)} %all-gather.2.cloned.1.call-done, f32[3072]{0:T(1024)S(1)} %get-tuple-element.11), kind=kOutput, calls=%fused_computation.19 | convolution fusion | flops 4865654784 | bytes 19673088 | tf_op jit(solution)/shard_map/dot_general | solution.py:126
  222.2 7.0 %convolution_convert_fusion = bf16[2048,3072]{1,0:T(8,128)(2,1)S(1)} fusion(bf16[2048,384]{1,0:T(8,128)(2,1)S(1)} %fusion.16, bf16[3072,384]{1,0:T(8,128)(2,1)S(1)} %copy-done), kind=kOutput, calls=%fused_computation.1 | convolution fusion | flops 4838129664 | bytes 16515072 | tf_op jit(solution)/shard_map/dot_general | solution.py:126
  229.3 5.4 copy.26
  236.0 10.8 %fusion.7 = bf16[3072,384]{1,0:T(8,128)(2,1)} fusion(bf16[2048,384]{1,0:T(8,128)(2,1)S(1)} %copy-done.10, bf16[2048,6144]{1,0:T(8,128)(2,1)} %all-gather.2.cloned.1.call-done), kind=kOutput, calls=%fused_computation.12 | convolution fusion | flops 4833017856 | bytes 16515072 | tf_op jit(solution)/shard_map/dot_general | solution.py:126
  246.8 3.2 reshape_reshape.7
  250.1 13.4 %fusion.6 = bf16[384,3072]{1,0:T(8,128)(2,1)S(1)} fusion(bf16[2048,6144]{1,0:T(8,128)(2,1)} %all-gather.2.cloned.1.call-done, f32[3072]{0:T(1024)S(1)} %get-tuple-element.11, f32[2048,384]{1,0:T(8,128)} %copy-done.11), kind=kOutput, calls=%fused_computation.11 | convolution fusion | flops 4858970112 | bytes 18100224 | tf_op jit(solution)/shard_map/dot_general | solution.py:126
  265.7 10.4 %pad_maximum_fusion = bf16[8,294912]{1,0:T(8,128)(2,1)} fusion(bf16[8,147456]{1,0:T(8,128)(2,1)} %bitcast.133, bf16[8,147456]{1,0:T(8,128)(2,1)S(1)} %reshape_reshape.7), kind=kLoop, calls=%fused_computation.10 | loop fusion | flops 9437184 | bytes 9437184 | tf_op jit(solution)/shard_map/concatenate | solution.py:64
  276.1 6.6 %reshape.116 = bf16[18432,128]{1,0:T(8,128)(2,1)} reshape(bf16[8,294912]{1,0:T(8,128)(2,1)} %pad_maximum_fusion) | data formatting | bytes 9437184 | tf_op jit(solution)/shard_map/reshape | solution.py:66
  282.8 79.7 %reduce-scatter.6.cloned.1.call-done = bf16[1,128,3072]{2,1,0:T(8,128)(2,1)} async-done(((bf16[8,128,3072]{2,1,0:T(8,128)(2,1)}), bf16[1,128,3072]{2,1,0:T(8,128)(2,1)}) %reduce-scatter.6.cloned.1.call-update) | async-done | bytes 786448 | tf_op jit(solution)/shard_map/reduce_scatter | solution.py:58
  364.1 2.5 fusion.29
  366.8 11.9 %all_to_all.26 = bf16[16,1,8,256]{3,2,1,0:T(8,128)(2,1)S(1)} all-to-all(bf16[16,1,8,256]{3,2,1,0:T(8,128)(2,1)S(1)} %constant_dynamic-update-slice_fusion.9), channel_id=1, replica_groups=mesh['dp'=8,'sp_0'=4,'sp_1'=2,'sp_2'=2] {'sp_0','sp_1','sp_2'}, dimensions={0} | all-to-all | bytes 131072 | tf_op jit(solution)/shard_map/all_to_all | solution.py:197
  379.3 10.0 %all_to_all.27 = f32[16,1,64]{2,1,0:T(1,128)S(1)} all-to-all(f32[16,1,64]{2,1,0:T(1,128)S(1)} %broadcast_in_dim.18), channel_id=1, replica_groups=mesh['dp'=8,'sp_0'=4,'sp_1'=2,'sp_2'=2] {'sp_0','sp_1','sp_2'}, dimensions={0} | all-to-all | bytes 8192 | tf_op jit(solution)/shard_map/all_to_all | solution.py:21
  391.1 31.1 %reduce-scatter.8.cloned.1.call-done = bf16[2304,128]{1,0:T(8,128)(2,1)} async-done(((bf16[18432,128]{1,0:T(8,128)(2,1)}), bf16[2304,128]{1,0:T(8,128)(2,1)}) %reduce-scatter.8.cloned.1.call-update) | async-done | bytes 589840 | tf_op jit(solution)/shard_map/reduce_scatter | solution.py:67
  425.3 154.6 %all-reduce.3.cloned.1.call-done = f32[1152,256]{1,0:T(8,128)} async-done(((f32[1152,256]{1,0:T(8,128)}), f32[1152,256]{1,0:T(8,128)}) %all-reduce.3.cloned.1.call-update) | async-done | bytes 1179664 | tf_op jit(solution)/shard_map/psum | solution.py:226
  579.9 2.4 copy.66
  (117 shorter events, 21.3 us)
Async XLA Ops:
  7.2 193.0 %copy-start = (bf16[3072,384]{1,0:T(8,128)(2,1)S(1)}, bf16[3072,384]{1,0:T(8,128)(2,1)}, u32[]{:S(2)}) copy-start(bf16[3072,384]{1,0:T(8,128)(2,1)} %param.16) | copy-start | bytes 7077892
  8.3 7.7 %collective-permute-start = (bf16[32,128]{1,0:T(8,128)(2,1)S(1)}, bf16[32,128]{1,0:T(8,128)(2,1)S(1)}, u32[]{:S(2)}, u32[]{:S(2)}) collective-permute-start(bf16[32,128]{1,0:T(8,128)(2,1)S(1)} %slice_bitcast_fusion), channel_id=1, source_target_pairs={{0,1},{1,2},{2,3},{3,4},{4,5},{5,6},{6,7},{7,8},{8,9},{9,10},{10,1... | collective-permute-start | bytes 24584 | tf_op jit(solution)/shard_map/ppermute | solution.py:16
  18.5 17.8 %copy-start.6 = (f32[256]{0:T(256)S(1)}, f32[256]{0:T(256)}, u32[]{:S(2)}) copy-start(f32[256]{0:T(256)} %param.13) | copy-start | bytes 3076
  18.5 17.8 %copy-start.7 = (f32[256]{0:T(256)S(1)}, f32[256]{0:T(256)}, u32[]{:S(2)}) copy-start(f32[256]{0:T(256)} %param.12) | copy-start | bytes 3076
  21.0 14.8 %all-to-all-start = ((f32[16,1,64]{2,1,0:T(1,128)}), f32[16,1,64]{2,1,0:T(1,128)S(1)}, u32[]{:S(2)}, u32[]{:S(2)}) async-start(f32[16,1,64]{2,1,0:T(1,128)} %broadcast_in_dim.15), calls=%async_computation | async-start | bytes 16384 | tf_op jit(solution)/shard_map/all_to_all | solution.py:21
  37.0 11.4 %all-to-all-start.1 = ((bf16[16,8,256]{2,1,0:T(8,128)(2,1)}), bf16[16,8,256]{2,1,0:T(8,128)(2,1)S(1)}, u32[]{:S(2)}, u32[]{:S(2)}) async-start(bf16[16,8,256]{2,1,0:T(8,128)(2,1)} %fusion.52), calls=%async_computation.1 | async-start | bytes 131072 | tf_op jit(solution)/shard_map/all_to_all | solution.py:158
  41.0 159.2 %all-gather.2.cloned.1.call-start = ((), (), s32[]{:S(2)}) async-start(), calls=%async_computation.7 | async-start | bytes 26738688 | tf_op jit(solution)/shard_map/all_gather | solution.py:40
  48.4 3.5 copy-start.4
  50.4 1.2 copy-start.2
  53.3 212.1 %reduce-scatter.4.cloned.1.call-start = ((), (), s32[]{:S(2)}) async-start(), calls=%async_computation.8 | async-start | bytes 18874368 | tf_op jit(solution)/shard_map/reduce_scatter | solution.py:57
  200.1 9.8 %copy-start.8 = (bf16[384,3072]{1,0:T(8,128)(2,1)S(1)}, bf16[384,3072]{1,0:T(8,128)(2,1)}, u32[]{:S(2)}) copy-start(bf16[384,3072]{1,0:T(8,128)(2,1)} %param.17) | copy-start | bytes 7077892
  209.9 12.3 %copy-start.11 = (f32[2048,384]{1,0:T(8,128)}, f32[2048,384]{1,0:T(8,128)S(1)}, u32[]{:S(2)}) copy-start(f32[2048,384]{1,0:T(8,128)S(1)} %fusion.2) | copy-start | bytes 9437188
  222.2 7.0 %copy-start.9 = (bf16[2048,384]{1,0:T(8,128)(2,1)}, bf16[2048,384]{1,0:T(8,128)(2,1)S(1)}, u32[]{:S(2)}) copy-start(bf16[2048,384]{1,0:T(8,128)(2,1)S(1)} %fusion.16) | copy-start | bytes 4718596
  234.6 1.4 copy-start.10
  234.7 127.8 %reduce-scatter.6.cloned.1.call-start = ((), (), s32[]{:S(2)}) async-start(), calls=%async_computation.9 | async-start | bytes 7077888 | tf_op jit(solution)/shard_map/reduce_scatter | solution.py:58
  265.4 156.8 %reduce-scatter.8.cloned.1.call-start = ((), (), s32[]{:S(2)}) async-start(), calls=%async_computation.11 | async-start | bytes 5308416 | tf_op jit(solution)/shard_map/reduce_scatter | solution.py:67
  282.7 79.8 %copy-start.3 = (f32[128,3072]{1,0:T(8,128)S(1)}, f32[128,3072]{1,0:T(8,128)}, u32[]{:S(2)}) copy-start(f32[128,3072]{1,0:T(8,128)} %copy-done.2) | copy-start | bytes 4718596
  282.7 81.4 %copy-start.5 = (bf16[1,128,3072]{2,1,0:T(8,128)(2,1)S(1)}, bf16[1,128,3072]{2,1,0:T(8,128)(2,1)}, u32[]{:S(2)}) copy-start(bf16[1,128,3072]{2,1,0:T(8,128)(2,1)} %param.19) | copy-start | bytes 2359300
  282.7 297.1 %all-reduce.3.cloned.1.call-start = ((), (), s32[]{:S(2)}) async-start(), calls=%async_computation.10 | async-start | bytes 2359296 | tf_op jit(solution)/shard_map/psum | solution.py:226
  391.1 191.1 %copy-start.1 = (bf16[3072,384]{1,0:T(8,128)(2,1)S(1)}, bf16[3072,384]{1,0:T(8,128)(2,1)}, u32[]{:S(2)}) copy-start(bf16[3072,384]{1,0:T(8,128)(2,1)} %param.16) | copy-start | bytes 7077892
Sparse Core Ops, SparseCore 0:
  53.4 146.6 all-gather.1
  234.8 21.5 reduce-scatter.3
  265.5 96.9 reduce-scatter.5
  364.9 57.2 reduce-scatter.7
  428.1 151.7 all-reduce.2
